TPU v7x, 32 devices: a whole 2x2x4 slice. The times are simulated.
32 devices in a mesh: expo: 4 (over y, x), fp: 8 (over z, core).
Axes of the slice: x: 2, y: 2, z: 4, core: 2. Of those that a mesh axis runs over, the one named last changes fastest.
Arguments:
- raw_pixels: bfloat16 [4, 2048, 2048], P('expo', 'fp'), may hold values from -6 to 6
- kernel_bank: bfloat16 [8, 2, 41], replicated, may hold values from -1 to 1
- kernel_ids: int32 [4, 8], P('expo', 'fp'), may hold values from 0 to 7
- inv_var: float32 [4, 8], P('expo', 'fp'), may hold values from 0.3 to 3
- gap_start: int32 [4, 8], P('expo', 'fp'), may hold values from 0 to 224
- warp_tile: int32 [4, 2048, 16, 1], P('expo', 'fp'), may hold values from 0 to 31; in each aligned block of 4096 rows (0 to 4095, 4096 to 8191, ..., all dimensions but the last counted through in order) at most 256 rows name the same one
- warp_offset: int32 [4, 2048, 16], P('expo', 'fp'), may hold values from 0 to 4095
Outputs:
- coadd_image: float32 [32, 4096, 128], P(('expo', 'fp'))
- coadd_weight: float32 [32, 4096], P(('expo', 'fp'))
Inputs may be any that keep to these rules, and one draw needn't show every extreme that they name: `warp_tile`: among the 4096 row segments of one exposure's CCD window (256 pixel rows of 16 segments each), at most 256 go to one tile, and in some windows exactly 256 do.
All inputs are finite; a program needn't handle non-finite values.
Results may differ from a plain program's by a relative error of at most 0.006.
Values may be sent and summed in bfloat16 or wider, within the bound.
No kernel may reach another device: no remote copies, remote signals or barrier semaphores. Data moves between devices by JAX's collectives and lax.ppermute only.
A program may use at most 64 MiB of HBM per device.

v0:
```python
import functools

import jax
import jax.numpy as jnp
from jax import lax
from jax.experimental import pallas as pl
from jax.experimental.pallas import tpu as pltpu
from jax.sharding import PartitionSpec as P


GAP = 32
EDGE = 32
LANES = 128
META = 8
GROUP = 8


VMEM = pl.BlockSpec(memory_space=pltpu.VMEM)
ANY = pl.BlockSpec(memory_space=pl.ANY)
f32, bf16, i32 = jnp.float32, jnp.bfloat16, jnp.int32


def iota(shape, dim):
    return lax.broadcasted_iota(i32, shape, dim)


def dot_last(a, b):
    return lax.dot_general(a, b, (((1,), (1,)), ((), ())), preferred_element_type=f32)


def near(x):
    return pltpu.with_memory_space_constraint(x, pltpu.VMEM)


def far(x):
    return pltpu.with_memory_space_constraint(x, pltpu.HBM)


def params(mib):
    return pltpu.CompilerParams(vmem_limit_bytes=mib << 20)


def cost(flops, moved):
    return pl.CostEstimate(flops=flops, bytes_accessed=moved, transcendentals=0)


def halo(shard, axis):
    size = lax.axis_size(axis)
    up = [(i, i + 1) for i in range(size - 1)]
    down = [(i + 1, i) for i in range(size - 1)]
    above = lax.ppermute(shard[-EDGE:], axis, up)
    below = lax.ppermute(shard[:EDGE], axis, down)
    return above, below


def route_kernel(capacity, tile_ref, off_ref, gap_ref, var_ref, id_ref, bank_ref, dest_ref, meta_ref, tv_ref, th_ref, line_ref):
    segs, rows = off_ref.shape
    devices = meta_ref.shape[0] // META
    parts = -(-capacity // LANES)
    gap, var, which_bank = gap_ref[...], var_ref[...], id_ref[...]
    bank = bank_ref[...].astype(f32)
    chosen = jnp.where(which_bank == 0, bank[0], 0.0)
    for k in range(1, bank.shape[0]):
        chosen = jnp.where(which_bank == k, bank[k], chosen)
    taps = bank.shape[2]
    half = taps // 2
    lead = -half % 8
    line_ref[...] = jnp.zeros(line_ref.shape, f32)
    line_ref[:, lead : lead + taps] = chosen
    for ref, which, shift in ((tv_ref, 0, EDGE - half), (th_ref, 1, LANES - half)):
        height, width = ref.shape
        wide = jnp.broadcast_to(line_ref[which : which + 1, :width], (height, width))
        ref[...] = pltpu.roll(wide, shift - lead, 1, stride=1, stride_axis=0).astype(bf16)
    line = iota((1, rows), 1)
    kept = jnp.logical_or(line < gap, line >= gap + GAP)
    before = (iota((rows, rows), 0) < iota((rows, rows), 1)).astype(bf16)
    owner = iota((devices, rows), 0)
    owner8 = iota((devices * META, rows), 0) >> 3
    field = iota((META, rows), 0)
    place = iota((LANES, rows), 0)
    base = jnp.zeros((devices, 1), f32)
    packed = jnp.zeros((devices * META, LANES), f32)
    for s in range(segs):
        tile = jnp.where(kept, tile_ref[s], -1)
        hot = (tile == owner).astype(f32)
        prefix = jnp.dot(hot.astype(bf16), before, preferred_element_type=f32)
        rank = jnp.sum(hot * (prefix + base), axis=0, keepdims=True).astype(i32)
        base = base + jnp.sum(hot, axis=1, keepdims=True)
        dest = jnp.where(kept, tile * capacity + rank, devices * capacity)
        for h in range(rows // LANES):
            dest_ref[s * (rows // LANES) + h] = dest[:, h * LANES : (h + 1) * LANES]
        offset = off_ref[s : s + 1, :]
        part = rank >> 7
        value = jnp.where(field == part, (offset >> 6) + 1, 0)
        value = jnp.where(field == part + parts, offset & 63, value).astype(f32)
        spread = jnp.concatenate([value] * devices, axis=0)
        stack = jnp.where(tile == owner8, spread, 0.0).astype(bf16)
        spot = (place == (rank & (LANES - 1))).astype(bf16)
        packed = packed + dot_last(stack, spot)
    first = var.astype(bf16).astype(f32)
    second = (var - first).astype(bf16).astype(f32)
    third = var - first - second
    row = iota((devices * META, LANES), 0) & (META - 1)
    packed = jnp.where(row == 4, first, packed)
    packed = jnp.where(row == 5, second, packed)
    packed = jnp.where(row == 6, third, packed)
    meta_ref[...] = packed.astype(bf16)


def own_index():
    return lax.axis_index("expo") * lax.axis_size("fp") + lax.axis_index("fp")


def pack_kernel(raw_ref, above_ref, below_ref, tv_ref, th_ref, dest_ref, meta_ref, all_ref, keep_ref, give_ref, edged, vert, conv, spread, stage, sems, *tables):
    devices, extended, _ = all_ref.shape
    me = own_index()
    capacity0 = extended - META
    chips, capacity1, _ = keep_ref.shape
    capacity = capacity0 + capacity1
    rows, cols = raw_ref.shape
    copies = [
        pltpu.make_async_copy(above_ref, edged.at[pl.ds(0, EDGE)], sems.at[0]),
        pltpu.make_async_copy(raw_ref, edged.at[pl.ds(EDGE, rows)], sems.at[1]),
        pltpu.make_async_copy(below_ref, edged.at[pl.ds(EDGE + rows, EDGE)], sems.at[2]),
    ]
    for k, table in enumerate(tables):
        copies.append(pltpu.make_async_copy(dest_ref.at[pl.ds(k, 1)], table, sems.at[3 + k]))
    for copy in copies:
        copy.start()
    vert[:, :LANES] = jnp.zeros((rows, LANES), bf16)
    vert[:, LANES + cols :] = jnp.zeros((rows, LANES), bf16)
    stage[:, capacity0:, :] = meta_ref[...].reshape(devices, META, LANES)
    for copy in copies:
        copy.wait()
    wide = 2 * LANES
    tall = rows + 2 * EDGE
    for c in range(cols // wide):
        part = jnp.dot(tv_ref[:, :tall], edged[:, c * wide : (c + 1) * wide], preferred_element_type=f32)
        vert[:, LANES + c * wide : LANES + (c + 1) * wide] = part.astype(bf16)
    for c in range(cols // wide):
        part = dot_last(vert[:, c * wide : c * wide + 2 * wide], th_ref[...])
        conv[2 * c * rows : (2 * c + 1) * rows, :] = part[:, :LANES]
        conv[(2 * c + 1) * rows : (2 * c + 2) * rows, :] = part[:, LANES:]

    def scatter(r, carry):
        for k, table in enumerate(tables):
            spread[pl.ds(table[0, 0, r], 1), :] = conv[pl.ds(r + k * LANES, 1), :]
        return carry

    lax.fori_loop(0, LANES, scatter, 0, unroll=2)

    def emit(k, carry):
        stage[k, :capacity0, :] = spread[pl.ds(pl.multiple_of(k * capacity, 8), capacity0), :].astype(bf16)
        return carry

    share = devices // 4
    copies = []
    for g in range(4):
        lax.fori_loop(g * share, (g + 1) * share, emit, 0)
        block = pl.ds(g * share, share)
        copies.append(pltpu.make_async_copy(stage.at[block], all_ref.at[block], sems.at[g]))
        copies[-1].start()
    for j in range(chips):
        for out, k in ((keep_ref, 2 * j), (give_ref, 2 * j + 1)):
            out[j] = spread[pl.ds(pl.multiple_of((me ^ k) * capacity + capacity0, 8), capacity1), :].astype(bf16)
    for copy in copies:
        copy.wait()


def join_kernel(keep_ref, take_ref, *outs):
    count = keep_ref.shape[1]
    for j, out in enumerate(outs):
        out[:count, :] = keep_ref[j]
        out[count:, :] = take_ref[j]


def add_rows(tables, scaled, sums, turns, count, first):
    member = iota((GROUP, LANES), 0)
    for p in sorted({p for _, p in tables}):
        low, high = max(first, p * LANES), min(first + count, (p + 1) * LANES)
        for turn in range(turns):

            def rank(r, carry):
                places = [tables[turn * GROUP + k, p][0, 0, r] for k in range(GROUP)]
                start = (r + (turn * count + p * LANES - first)) * GROUP
                fresh = scaled[pl.ds(pl.multiple_of(start, GROUP), GROUP), :]
                held = [acc[pl.ds(place, GROUP), :] for acc, place in zip(sums, places)]
                for k in range(GROUP):
                    sums[k][pl.ds(places[k], GROUP), :] = held[k] + jnp.where(member == k, fresh, 0.0)
                return carry

            lax.fori_loop(low - p * LANES, high - p * LANES, rank, 0, unroll=8)


def first_kernel(slots, parts, values_ref, *refs):
    (spots, factors, weight_out), refs = refs[:3], refs[3:]
    sums, (scaled, shifted, sems), refs = refs[:GROUP], refs[GROUP : GROUP + 3], refs[GROUP + 3 :]
    devices, extended, _ = values_ref.shape
    count = extended - META
    used = -(-count // LANES)
    tables = {(n, p): refs[n * used + p] for n in range(devices) for p in range(used)}
    high_id = iota((slots // LANES, LANES), 0)
    low_id = iota((LANES, LANES), 0)
    weight = jnp.zeros((slots // LANES, LANES), f32)
    share = sums[0].shape[0] // devices
    copies = []
    for n in range(devices):
        turn, member = divmod(n, GROUP)
        for acc in sums:
            acc[n * share : (n + 1) * share, :] = jnp.zeros((share, LANES), f32)
        fields = values_ref[n, count:, :].astype(f32)
        factor = fields[4:5, :] + fields[5:6, :] + fields[6:7, :]
        factors[n] = factor
        for p in range(parts):
            high, low = fields[p : p + 1, :], fields[parts + p : parts + p + 1, :]
            slot = jnp.where(high > 0.5, (high - 1.0) * 64.0 + low, float(slots)).astype(i32)
            spots[n * parts + p] = slot
            if p < used:
                shifted[n * used + p] = slot + (GROUP - member)
            high = ((slot >> 7) == high_id).astype(bf16)
            low = ((slot & (LANES - 1)) == low_id).astype(bf16)
            weight = weight + factor * dot_last(high, low)
        scaled[pl.ds(turn * count * GROUP + member, count, stride=GROUP), :] = values_ref[n, :count, :].astype(f32) * factor
    for k, table in enumerate(tables.values()):
        copies.append(pltpu.make_async_copy(shifted.at[pl.ds(k, 1)], table, sems.at[k]))
        copies[-1].start()
    weight_out[...] = weight
    for copy in copies:
        copy.wait()
    add_rows(tables, scaled, sums, devices // GROUP, count, 0)


def rest_kernel(low, high, first, parts, closes, *refs):
    chips = high - low
    pairs, (spots, factors), refs = refs[:chips], refs[chips : chips + 2], refs[chips + 2 :]
    weight_in, refs = (refs[0], refs[1:]) if closes else (None, refs)
    refs = refs[GROUP:]
    (image_ref, weight_ref), refs = (refs[:2], refs[2:]) if closes else ((None, None), refs)
    sums, (scaled, shifted, sems), refs = refs[:GROUP], refs[GROUP : GROUP + 3], refs[GROUP + 3 :]
    stage, refs = (refs[0], refs[1:]) if closes else (None, refs)
    count = pairs[0].shape[0] // 2
    me = own_index()
    begin = first // LANES
    used = parts - begin
    sources = 2 * chips
    tables = {(n, begin + p): refs[n * used + p] for n in range(sources) for p in range(used)}
    copies = []
    if closes:
        copies.append(pltpu.make_async_copy(weight_in, weight_ref, sems.at[len(tables)]))
        copies[0].start()
    for k, (n, p) in enumerate(tables):
        shifted[k] = spots[(me ^ (2 * low + n)) * parts + p] + (GROUP - n % GROUP)
    for k, table in enumerate(tables.values()):
        copies.append(pltpu.make_async_copy(shifted.at[pl.ds(k, 1)], table, sems.at[k]))
        copies[-1].start()
    for n in range(sources):
        turn, member = divmod(n, GROUP)
        rows = pairs[n // 2][n % 2 * count : (n % 2 + 1) * count, :].astype(f32)
        scaled[pl.ds(turn * count * GROUP + member, count, stride=GROUP), :] = rows * factors[me ^ (2 * low + n)]
    for copy in copies:
        copy.wait()
    add_rows(tables, scaled, sums, sources // GROUP, count, first)
    if not closes:
        return
    weight = weight_in[...]

    def mean(h, total):
        scale = jnp.broadcast_to(jnp.maximum(weight[h : h + 1, :], 1.0), (LANES, LANES)).T
        return total / scale

    merge(sums, stage, mean, image_ref, sems)


def merge(sums, stage, finish, out_ref, sems):
    copies = []
    blocks = stage.shape[0] // LANES
    quarter = blocks // 4
    for h in range(blocks):
        total = [acc[GROUP + h * LANES : GROUP + (h + 1) * LANES, :] for acc in sums]
        while len(total) > 1:
            total = [a + b for a, b in zip(total[::2], total[1::2])] + total[len(total) // 2 * 2 :]
        stage[h * LANES : (h + 1) * LANES, :] = finish(h, total[0])
        if h % quarter == quarter - 1:
            ready = pl.ds((h + 1 - quarter) * LANES, quarter * LANES)
            copies.append(pltpu.make_async_copy(stage.at[ready], out_ref.at[ready], sems.at[h // quarter]))
            copies[-1].start()
    for copy in copies:
        copy.wait()


def body(raw_pixels, kernel_bank, kernel_ids, inv_var, gap_start, warp_tile, warp_offset):
    _, rows, cols = raw_pixels.shape
    segs = cols // LANES
    axes = ("expo", "fp")
    devices = lax.axis_size("expo") * lax.axis_size("fp")
    pieces = rows * segs
    capacity = 2 * pieces // devices
    parts = -(-capacity // LANES)
    slots = pieces

    raw = raw_pixels[0]
    above, below = halo(raw, "fp")
    tiles = jnp.transpose(warp_tile[0], (1, 2, 0))
    offsets = jnp.transpose(warp_offset[0], (1, 0))
    tall = -(-(rows + 2 * EDGE) // LANES) * LANES
    dest, meta, tv, th = pl.pallas_call(
        functools.partial(route_kernel, capacity),
        out_shape=(
            pltpu.VMEM((pieces // LANES, 1, LANES), i32),
            pltpu.VMEM((devices * META, LANES), bf16),
            pltpu.VMEM((rows, tall), bf16),
            pltpu.VMEM((2 * LANES, 4 * LANES), bf16),
        ),
        in_specs=[VMEM] * 6,
        out_specs=(VMEM,) * 4,
        scratch_shapes=[pltpu.VMEM((2, 4 * LANES), f32)],
        cost_estimate=cost(400_000_000, 600_000),
        compiler_params=params(16),
        name="route",
    )(far(tiles), far(offsets), gap_start, inv_var, kernel_ids, far(kernel_bank))

    capacity1 = capacity // 2
    capacity0 = capacity - capacity1
    chips = devices // 2
    everything, keep, give = pl.pallas_call(
        pack_kernel,
        out_shape=(pltpu.HBM((devices, capacity0 + META, LANES), bf16),)
        + (pltpu.VMEM((chips, capacity1, LANES), bf16),) * 2,
        in_specs=[ANY, ANY, ANY, VMEM, VMEM, VMEM, VMEM],
        out_specs=(ANY, VMEM, VMEM),
        scratch_shapes=[
            pltpu.VMEM((rows + 2 * EDGE, cols), bf16),
            pltpu.VMEM((rows, cols + 2 * LANES), bf16),
            pltpu.VMEM((pieces, LANES), f32),
            pltpu.VMEM((devices * capacity + 8, LANES), f32),
            pltpu.VMEM((devices, capacity0 + META, LANES), bf16),
            pltpu.SemaphoreType.DMA((3 + pieces // LANES,)),
        ]
        + [pltpu.SMEM((1, 1, LANES), i32)] * (pieces // LANES),
        cost_estimate=cost(10_000_000_000, 4_000_000),
        compiler_params=params(20),
        name="pack",
    )(far(raw), near(above), near(below), near(tv), near(th), near(dest), near(meta))

    most = 8 * devices
    total = pltpu.VMEM((-(-(slots + 3 * GROUP) // most) * most, LANES), f32)
    got = lax.all_to_all(everything, axes, split_axis=0, concat_axis=0, tiled=True)
    take = lax.ppermute(give, axes, [(i, i ^ 1) for i in range(devices)])
    joined = pl.pallas_call(
        join_kernel,
        out_shape=(pltpu.VMEM((2 * capacity1, LANES), bf16),) * chips,
        in_specs=[VMEM, VMEM],
        out_specs=(VMEM,) * chips,
        cost_estimate=cost(1_000_000, 1_000_000),
        compiler_params=params(2),
        name="join",
    )(near(keep), near(take))
    rest = [joined[0]]
    cuts = (0, chips // 2, chips * 3 // 4, chips)
    for low, high in zip(cuts, cuts[1:]):
        for j in range(max(low, 1), high):
            rest.append(lax.ppermute(joined[j], axes, [(i, i ^ (2 * j)) for i in range(devices)]))

    used = -(-capacity0 // LANES)
    spots, factors, weight, *sums = pl.pallas_call(
        functools.partial(first_kernel, slots, parts),
        out_shape=(
            pltpu.VMEM((devices * parts, 1, LANES), i32),
            pltpu.VMEM((devices, 1, LANES), f32),
            pltpu.VMEM((slots // LANES, LANES), f32),
        )
        + (total,) * GROUP,
        in_specs=[VMEM],
        out_specs=(VMEM,) * (3 + GROUP),
        scratch_shapes=[
            pltpu.VMEM((devices * capacity0, LANES), f32),
            pltpu.VMEM((devices * used, 1, LANES), i32),
            pltpu.SemaphoreType.DMA((devices * used,)),
        ]
        + [pltpu.SMEM((1, 1, LANES), i32)] * (devices * used),
        cost_estimate=cost(4_000_000_000, 8_000_000),
        compiler_params=params(8),
        name="sum_first",
    )(near(got))
    used = parts - capacity0 // LANES
    for low, high in zip(cuts, cuts[1:]):
        closes = high == chips
        number, here = high - low, 2 * (high - low)
        ends = (pltpu.HBM((slots, LANES), f32), pltpu.HBM((slots // LANES, LANES), f32)) if closes else ()
        lead = number + 2 + closes
        out = pl.pallas_call(
            functools.partial(rest_kernel, low, high, capacity0, parts, closes),
            out_shape=ends + (total,) * GROUP,
            in_specs=[VMEM] * (lead + GROUP),
            out_specs=(ANY,) * len(ends) + (VMEM,) * GROUP,
            scratch_shapes=[
                pltpu.VMEM((here * capacity1, LANES), f32),
                pltpu.VMEM((here * used, 1, LANES), i32),
                pltpu.SemaphoreType.DMA((here * used + 1,)),
            ]
            + [pltpu.VMEM((slots, LANES), f32)] * closes
            + [pltpu.SMEM((1, 1, LANES), i32)] * (here * used),
            input_output_aliases={lead + k: len(ends) + k for k in range(GROUP)},
            cost_estimate=cost(4_000_000_000, 8_000_000),
            compiler_params=params(8),
        )(
            *[near(x) for x in rest[low:high]],
            near(spots),
            near(factors),
            *[near(weight)] * closes,
            *[near(x) for x in sums],
        )
        sums = out[len(ends) :]
    image, weight = out[:2]
    return image[None], weight.reshape(1, slots)


def solution(mesh):
    in_specs = (
        P("expo", "fp", None),
        P(),
        P("expo", "fp"),
        P("expo", "fp"),
        P("expo", "fp"),
        P("expo", "fp", None, None),
        P("expo", "fp", None),
    )
    out_specs = (P(("expo", "fp"), None, None), P(("expo", "fp"), None))
    return jax.shard_map(body, mesh=mesh, in_specs=in_specs, out_specs=out_specs, check_vma=False)
```

profile of v0, /device:TPU:0, one launch (start us, length us, event | category | flops | bytes accessed | tf_op | source)
XLA Modules:
  0.0 96.2 jit_solution(14697849053191702228)
XLA Ops:
  0.6 1.0 %slice_bitcast_fusion = (bf16[32,2048]{1,0:T(8,128)(2,1)S(1)}, bf16[32,2048]{1,0:T(8,128)(2,1)S(1)}) fusion(bf16[1,256,2048]{2,1,0:T(8,128)(2,1)} %param.7), kind=kLoop, calls=%fused_computation | loop fusion | bytes 524288 | tf_op jit(solution)/shard_map/slice | solution.py:52
  1.6 1.3 %collective-permute-start.1 = (bf16[32,2048]{1,0:T(8,128)(2,1)S(1)}, bf16[32,2048]{1,0:T(8,128)(2,1)S(1)}, u32[]{:S(2)}, u32[]{:S(2)}) collective-permute-start(bf16[32,2048]{1,0:T(8,128)(2,1)S(1)} %get-tuple-element.106), channel_id=1, source_target_pairs={{1,0},{2,1},{3,2},{4,3},{5,4},{6,5},{7,6},{9,8},{10,9},{11,10},{12... | collective-permute-start | bytes 393224 | tf_op jit(solution)/shard_map/ppermute | solution.py:52
  2.9 3.0 %collective-permute-start = (bf16[32,2048]{1,0:T(8,128)(2,1)S(1)}, bf16[32,2048]{1,0:T(8,128)(2,1)S(1)}, u32[]{:S(2)}, u32[]{:S(2)}) collective-permute-start(bf16[32,2048]{1,0:T(8,128)(2,1)S(1)} %get-tuple-element.107), channel_id=1, source_target_pairs={{0,1},{1,2},{2,3},{3,4},{4,5},{5,6},{6,7},{8,9},{9,10},{10,11},{11... | collective-permute-start | bytes 393224 | tf_op jit(solution)/shard_map/ppermute | solution.py:51
  7.9 2.8 %route.1 = (s32[32,1,128]{2,1,0:T(1,128)S(1)}, bf16[256,128]{1,0:T(8,128)(2,1)S(1)}, bf16[256,384]{1,0:T(8,128)(2,1)S(1)}, bf16[256,512]{1,0:T(8,128)(2,1)S(1)}) custom-call(s32[16,1,256]{2,1,0:T(1,128)} %bitcast.15, s32[16,256]{1,0:T(8,128)} %bitcast.16, s32[1,1]{1,0:T(1,128)S(6)} %copy.59.gap_ref, f32[1,1]{1,0:T(1,128)S(6)} %copy.58.var_ref, ...), custom_call_target="tpu_custom_call" | custom-call | flops 400000000 | bytes 600000 | tf_op jit(solution)/shard_map/route/pallas_call | solution.py:306
  10.7 0.0 collective-permute-done.1.below_ref
  10.7 0.0 collective-permute-done.above_ref
  10.7 6.8 %pack.1 = (bf16[32,136,128]{2,1,0:T(8,128)(2,1)}, bf16[16,128,128]{2,1,0:T(8,128)(2,1)S(1)}, bf16[16,128,128]{2,1,0:T(8,128)(2,1)S(1)}) custom-call(bf16[256,2048]{1,0:T(8,128)(2,1)} %bitcast.13, bf16[32,2048]{1,0:T(8,128)(2,1)S(1)} %collective-permute-done.above_ref, bf16[32,2048]{1,0:T(8,128)(2,1)S(1)} %collective-permute-done.1.below_ref, ...), custom_call_target="tpu_custom_call" | custom-call | flops 10000000000 | bytes 4000000 | tf_op jit(solution)/shard_map/pack/pallas_call | solution.py:325
  17.5 7.3 %all-to-all-start = ((bf16[32,136,128]{2,1,0:T(8,128)(2,1)}), bf16[32,136,128]{2,1,0:T(8,128)(2,1)S(1)}, u32[]{:S(2)}, u32[]{:S(2)}) async-start(bf16[32,136,128]{2,1,0:T(8,128)(2,1)} %get-tuple-element.64), calls=%async_computation | async-start | bytes 2228224 | tf_op jit(solution)/shard_map/all_to_all | solution.py:347
  24.9 0.3 collective-permute-start.2
  25.2 1.7 %collective-permute-done.2.take_ref = bf16[16,128,128]{2,1,0:T(8,128)(2,1)S(1)} collective-permute-done((bf16[16,128,128]{2,1,0:T(8,128)(2,1)S(1)}, bf16[16,128,128]{2,1,0:T(8,128)(2,1)S(1)}, u32[]{:S(2)}, u32[]{:S(2)}) %collective-permute-start.2) | collective-permute-done | bytes 524320 | tf_op jit(solution)/shard_map/ppermute | solution.py:348
  26.9 0.1 join.1
  26.9 1.8 %collective-permute-start.11 = (bf16[256,128]{1,0:T(8,128)(2,1)S(1)}, bf16[256,128]{1,0:T(8,128)(2,1)S(1)}, u32[]{:S(2)}, u32[]{:S(2)}) collective-permute-start(bf16[256,128]{1,0:T(8,128)(2,1)S(1)} %get-tuple-element.73), channel_id=1, source_target_pairs={{0,2},{1,3},{2,0},{3,1},{4,6},{5,7},{6,4},{7,5},{8,10},{9,11},{10,... | collective-permute-start | bytes 196616 | tf_op jit(solution)/shard_map/ppermute | solution.py:362
  28.8 2.4 %collective-permute-start.12 = (bf16[256,128]{1,0:T(8,128)(2,1)S(1)}, bf16[256,128]{1,0:T(8,128)(2,1)S(1)}, u32[]{:S(2)}, u32[]{:S(2)}) collective-permute-start(bf16[256,128]{1,0:T(8,128)(2,1)S(1)} %get-tuple-element.74), channel_id=1, source_target_pairs={{0,4},{1,5},{2,6},{3,7},{4,0},{5,1},{6,2},{7,3},{8,12},{9,13},{10,... | collective-permute-start | bytes 196616 | tf_op jit(solution)/shard_map/ppermute | solution.py:362
  31.2 0.2 collective-permute-start.13
  31.4 1.8 %collective-permute-start.14 = (bf16[256,128]{1,0:T(8,128)(2,1)S(1)}, bf16[256,128]{1,0:T(8,128)(2,1)S(1)}, u32[]{:S(2)}, u32[]{:S(2)}) collective-permute-start(bf16[256,128]{1,0:T(8,128)(2,1)S(1)} %get-tuple-element.76), channel_id=1, source_target_pairs={{0,8},{1,9},{2,10},{3,11},{4,12},{5,13},{6,14},{7,15},{8,0},{9,1},... | collective-permute-start | bytes 196616 | tf_op jit(solution)/shard_map/ppermute | solution.py:362
  33.2 0.6 collective-permute-start.15
  33.7 11.5 %collective-permute-done.11.refs_1_ = bf16[256,128]{1,0:T(8,128)(2,1)S(1)} collective-permute-done((bf16[256,128]{1,0:T(8,128)(2,1)S(1)}, bf16[256,128]{1,0:T(8,128)(2,1)S(1)}, u32[]{:S(2)}, u32[]{:S(2)}) %collective-permute-start.11) | collective-permute-done | bytes 65568 | tf_op jit(solution)/shard_map/ppermute | solution.py:362
  45.2 5.7 %collective-permute-start.16 = (bf16[256,128]{1,0:T(8,128)(2,1)S(1)}, bf16[256,128]{1,0:T(8,128)(2,1)S(1)}, u32[]{:S(2)}, u32[]{:S(2)}) collective-permute-start(bf16[256,128]{1,0:T(8,128)(2,1)S(1)} %get-tuple-element.78), channel_id=1, source_target_pairs={{0,12},{1,13},{2,14},{3,15},{4,8},{5,9},{6,10},{7,11},{8,4},{9,5},... | collective-permute-start | bytes 196616 | tf_op jit(solution)/shard_map/ppermute | solution.py:362
  50.9 7.8 %collective-permute-done.12.refs_2_ = bf16[256,128]{1,0:T(8,128)(2,1)S(1)} collective-permute-done((bf16[256,128]{1,0:T(8,128)(2,1)S(1)}, bf16[256,128]{1,0:T(8,128)(2,1)S(1)}, u32[]{:S(2)}, u32[]{:S(2)}) %collective-permute-start.12) | collective-permute-done | bytes 65568 | tf_op jit(solution)/shard_map/ppermute | solution.py:362
  58.7 1.8 %collective-permute-start.17 = (bf16[256,128]{1,0:T(8,128)(2,1)S(1)}, bf16[256,128]{1,0:T(8,128)(2,1)S(1)}, u32[]{:S(2)}, u32[]{:S(2)}) collective-permute-start(bf16[256,128]{1,0:T(8,128)(2,1)S(1)} %get-tuple-element.79), channel_id=1, source_target_pairs={{0,14},{1,15},{2,12},{3,13},{4,10},{5,11},{6,8},{7,9},{8,6},{9,7},... | collective-permute-start | bytes 196616 | tf_op jit(solution)/shard_map/ppermute | solution.py:362
  60.5 0.0 all-to-all-done.values_ref
  60.5 6.8 %sum_first.1 = (s32[64,1,128]{2,1,0:T(1,128)S(1)}, f32[32,1,128]{2,1,0:T(1,128)S(1)}, f32[32,128]{1,0:T(8,128)S(1)}, f32[4352,128]{1,0:T(8,128)S(1)}, f32[4352,1...) custom-call(bf16[32,136,128]{2,1,0:T(8,128)(2,1)S(1)} %all-to-all-do, ...), custom_call_target="tpu_custom_call" | custom-call | flops 4000000000 | bytes 8000000 | tf_op jit(solution)/shard_map/sum_first/pallas_call | solution.py:365
  67.3 0.0 collective-permute-done.13.refs_3_
  67.3 2.2 %collective-permute-start.3 = (bf16[256,128]{1,0:T(8,128)(2,1)S(1)}, bf16[256,128]{1,0:T(8,128)(2,1)S(1)}, u32[]{:S(2)}, u32[]{:S(2)}) collective-permute-start(bf16[256,128]{1,0:T(8,128)(2,1)S(1)} %get-tuple-element.60), channel_id=1, source_target_pairs={{0,24},{1,25},{2,26},{3,27},{4,28},{5,29},{6,30},{7,31},{8,16},{9,... | collective-permute-start | bytes 196616 | tf_op jit(solution)/shard_map/ppermute | solution.py:362
  69.6 0.0 collective-permute-done.14.refs_4_
  69.6 0.2 collective-permute-start.7
  69.8 0.0 collective-permute-done.15.refs_5_
  69.8 0.0 collective-permute-start.8
  69.8 0.0 collective-permute-done.16.refs_6_
  69.8 4.7 %collective-permute-start.9 = (bf16[256,128]{1,0:T(8,128)(2,1)S(1)}, bf16[256,128]{1,0:T(8,128)(2,1)S(1)}, u32[]{:S(2)}, u32[]{:S(2)}) collective-permute-start(bf16[256,128]{1,0:T(8,128)(2,1)S(1)} %get-tuple-element.70), channel_id=1, source_target_pairs={{0,20},{1,21},{2,22},{3,23},{4,16},{5,17},{6,18},{7,19},{8,28},{9,... | collective-permute-start | bytes 196616 | tf_op jit(solution)/shard_map/ppermute | solution.py:362
  74.5 0.0 collective-permute-done.17.refs_7_
  74.5 1.8 %collective-permute-start.10 = (bf16[256,128]{1,0:T(8,128)(2,1)S(1)}, bf16[256,128]{1,0:T(8,128)(2,1)S(1)}, u32[]{:S(2)}, u32[]{:S(2)}) collective-permute-start(bf16[256,128]{1,0:T(8,128)(2,1)S(1)} %get-tuple-element.71), channel_id=1, source_target_pairs={{0,22},{1,23},{2,20},{3,21},{4,18},{5,19},{6,16},{7,17},{8,30},{9,... | collective-permute-start | bytes 196616 | tf_op jit(solution)/shard_map/ppermute | solution.py:362
  76.3 3.3 %shard_map.86 = (f32[4352,128]{1,0:T(8,128)S(1)}, f32[4352,128]{1,0:T(8,128)S(1)}, f32[4352,128]{1,0:T(8,128)S(1)}, f32[4352,128]{1,0:T(8,128)S(1)}, f32[4352,12...) custom-call(bf16[256,128]{1,0:T(8,128)(2,1)S(1)} %get-tuple-element., ...), custom_call_target="tpu_custom_call", output_to_operand_aliasing={{0}: (10, {}), {1}: (11, {}), {2}: (12, {}), {3}: (13, {}),... | custom-call | flops 4000000000 | bytes 8000000 | tf_op jit(solution)/shard_map/pallas_call | solution.py:391
  79.6 0.0 collective-permute-done.7.refs_0_
  79.6 0.1 collective-permute-start.4
  79.7 0.0 collective-permute-done.8.refs_1_
  79.7 5.2 %collective-permute-start.5 = (bf16[256,128]{1,0:T(8,128)(2,1)S(1)}, bf16[256,128]{1,0:T(8,128)(2,1)S(1)}, u32[]{:S(2)}, u32[]{:S(2)}) collective-permute-start(bf16[256,128]{1,0:T(8,128)(2,1)S(1)} %get-tuple-element.62), channel_id=1, source_target_pairs={{0,28},{1,29},{2,30},{3,31},{4,24},{5,25},{6,26},{7,27},{8,20},{9,... | collective-permute-start | bytes 196616 | tf_op jit(solution)/shard_map/ppermute | solution.py:362
  84.9 0.0 collective-permute-done.9.refs_2_
  84.9 1.3 %collective-permute-start.6 = (bf16[256,128]{1,0:T(8,128)(2,1)S(1)}, bf16[256,128]{1,0:T(8,128)(2,1)S(1)}, u32[]{:S(2)}, u32[]{:S(2)}) collective-permute-start(bf16[256,128]{1,0:T(8,128)(2,1)S(1)} %get-tuple-element.63), channel_id=1, source_target_pairs={{0,30},{1,31},{2,28},{3,29},{4,26},{5,27},{6,24},{7,25},{8,22},{9,... | collective-permute-start | bytes 196616 | tf_op jit(solution)/shard_map/ppermute | solution.py:362
  86.2 0.0 collective-permute-done.10.refs_3_
  86.2 1.9 %shard_map.87 = (f32[4352,128]{1,0:T(8,128)S(1)}, f32[4352,128]{1,0:T(8,128)S(1)}, f32[4352,128]{1,0:T(8,128)S(1)}, f32[4352,128]{1,0:T(8,128)S(1)}, f32[4352,12...) custom-call(bf16[256,128]{1,0:T(8,128)(2,1)S(1)} %collective-permute, ...), custom_call_target="tpu_custom_call", output_to_operand_aliasing={{0}: (6, {}), {1}: (7, {}), {2}: (8, {}), {3}: (9, {}), {4}... | custom-call | flops 4000000000 | bytes 8000000 | tf_op jit(solution)/shard_map/pallas_call | solution.py:391
  88.0 0.0 collective-permute-done.3.refs_0_
  88.1 0.0 collective-permute-done.4.refs_1_
  88.1 0.5 collective-permute-done.5.refs_2_
  88.6 4.2 %collective-permute-done.6.refs_3_ = bf16[256,128]{1,0:T(8,128)(2,1)S(1)} collective-permute-done((bf16[256,128]{1,0:T(8,128)(2,1)S(1)}, bf16[256,128]{1,0:T(8,128)(2,1)S(1)}, u32[]{:S(2)}, u32[]{:S(2)}) %collective-permute-start.6) | collective-permute-done | bytes 65568 | tf_op jit(solution)/shard_map/ppermute | solution.py:362
  92.8 3.5 %shard_map.88 = (f32[4096,128]{1,0:T(8,128)}, f32[32,128]{1,0:T(8,128)}, f32[4352,128]{1,0:T(8,128)S(1)}, f32[4352,128]{1,0:T(8,128)S(1)}, f32[4352,128]{1,0:T(8...) custom-call(bf16[256,128]{1,0:T(8,128)(2,1)S(1)} %collective-permute, ...), custom_call_target="tpu_custom_call", output_to_operand_aliasing={{2}: (7, {}), {3}: (8, {}), {4}: (9, {}), {5}: (10, {}), {6... | custom-call | flops 4000000000 | bytes 8000000 | tf_op jit(solution)/shard_map/pallas_call | solution.py:391
Async XLA Ops:
  1.6 9.1 %collective-permute-start.1 = (bf16[32,2048]{1,0:T(8,128)(2,1)S(1)}, bf16[32,2048]{1,0:T(8,128)(2,1)S(1)}, u32[]{:S(2)}, u32[]{:S(2)}) collective-permute-start(bf16[32,2048]{1,0:T(8,128)(2,1)S(1)} %get-tuple-element.106), channel_id=1, source_target_pairs={{1,0},{2,1},{3,2},{4,3},{5,4},{6,5},{7,6},{9,8},{10,9},{11,10},{12... | collective-permute-start | bytes 393224 | tf_op jit(solution)/shard_map/ppermute | solution.py:52
  2.9 7.8 %collective-permute-start = (bf16[32,2048]{1,0:T(8,128)(2,1)S(1)}, bf16[32,2048]{1,0:T(8,128)(2,1)S(1)}, u32[]{:S(2)}, u32[]{:S(2)}) collective-permute-start(bf16[32,2048]{1,0:T(8,128)(2,1)S(1)} %get-tuple-element.107), channel_id=1, source_target_pairs={{0,1},{1,2},{2,3},{3,4},{4,5},{5,6},{6,7},{8,9},{9,10},{10,11},{11... | collective-permute-start | bytes 393224 | tf_op jit(solution)/shard_map/ppermute | solution.py:51
  17.5 43.0 %all-to-all-start = ((bf16[32,136,128]{2,1,0:T(8,128)(2,1)}), bf16[32,136,128]{2,1,0:T(8,128)(2,1)S(1)}, u32[]{:S(2)}, u32[]{:S(2)}) async-start(bf16[32,136,128]{2,1,0:T(8,128)(2,1)} %get-tuple-element.64), calls=%async_computation | async-start | bytes 2228224 | tf_op jit(solution)/shard_map/all_to_all | solution.py:347
  24.9 2.0 %collective-permute-start.2 = (bf16[16,128,128]{2,1,0:T(8,128)(2,1)S(1)}, bf16[16,128,128]{2,1,0:T(8,128)(2,1)S(1)}, u32[]{:S(2)}, u32[]{:S(2)}) collective-permute-start(bf16[16,128,128]{2,1,0:T(8,128)(2,1)S(1)} %get-tuple-element.59), channel_id=1, source_target_pairs={{0,1},{1,0},{2,3},{3,2},{4,5},{5,4},{6,7},{7,6},{8,9},{9,8},{10,11... | collective-permute-start | bytes 1572872 | tf_op jit(solution)/shard_map/ppermute | solution.py:348
  26.9 18.3 %collective-permute-start.11 = (bf16[256,128]{1,0:T(8,128)(2,1)S(1)}, bf16[256,128]{1,0:T(8,128)(2,1)S(1)}, u32[]{:S(2)}, u32[]{:S(2)}) collective-permute-start(bf16[256,128]{1,0:T(8,128)(2,1)S(1)} %get-tuple-element.73), channel_id=1, source_target_pairs={{0,2},{1,3},{2,0},{3,1},{4,6},{5,7},{6,4},{7,5},{8,10},{9,11},{10,... | collective-permute-start | bytes 196616 | tf_op jit(solution)/shard_map/ppermute | solution.py:362
  28.8 29.9 %collective-permute-start.12 = (bf16[256,128]{1,0:T(8,128)(2,1)S(1)}, bf16[256,128]{1,0:T(8,128)(2,1)S(1)}, u32[]{:S(2)}, u32[]{:S(2)}) collective-permute-start(bf16[256,128]{1,0:T(8,128)(2,1)S(1)} %get-tuple-element.74), channel_id=1, source_target_pairs={{0,4},{1,5},{2,6},{3,7},{4,0},{5,1},{6,2},{7,3},{8,12},{9,13},{10,... | collective-permute-start | bytes 196616 | tf_op jit(solution)/shard_map/ppermute | solution.py:362
  31.2 36.1 %collective-permute-start.13 = (bf16[256,128]{1,0:T(8,128)(2,1)S(1)}, bf16[256,128]{1,0:T(8,128)(2,1)S(1)}, u32[]{:S(2)}, u32[]{:S(2)}) collective-permute-start(bf16[256,128]{1,0:T(8,128)(2,1)S(1)} %get-tuple-element.75), channel_id=1, source_target_pairs={{0,6},{1,7},{2,4},{3,5},{4,2},{5,3},{6,0},{7,1},{8,14},{9,15},{10,... | collective-permute-start | bytes 196616 | tf_op jit(solution)/shard_map/ppermute | solution.py:362
  31.4 38.2 %collective-permute-start.14 = (bf16[256,128]{1,0:T(8,128)(2,1)S(1)}, bf16[256,128]{1,0:T(8,128)(2,1)S(1)}, u32[]{:S(2)}, u32[]{:S(2)}) collective-permute-start(bf16[256,128]{1,0:T(8,128)(2,1)S(1)} %get-tuple-element.76), channel_id=1, source_target_pairs={{0,8},{1,9},{2,10},{3,11},{4,12},{5,13},{6,14},{7,15},{8,0},{9,1},... | collective-permute-start | bytes 196616 | tf_op jit(solution)/shard_map/ppermute | solution.py:362
  33.2 36.6 %collective-permute-start.15 = (bf16[256,128]{1,0:T(8,128)(2,1)S(1)}, bf16[256,128]{1,0:T(8,128)(2,1)S(1)}, u32[]{:S(2)}, u32[]{:S(2)}) collective-permute-start(bf16[256,128]{1,0:T(8,128)(2,1)S(1)} %get-tuple-element.77), channel_id=1, source_target_pairs={{0,10},{1,11},{2,8},{3,9},{4,14},{5,15},{6,12},{7,13},{8,2},{9,3},... | collective-permute-start | bytes 196616 | tf_op jit(solution)/shard_map/ppermute | solution.py:362
  45.2 24.6 %collective-permute-start.16 = (bf16[256,128]{1,0:T(8,128)(2,1)S(1)}, bf16[256,128]{1,0:T(8,128)(2,1)S(1)}, u32[]{:S(2)}, u32[]{:S(2)}) collective-permute-start(bf16[256,128]{1,0:T(8,128)(2,1)S(1)} %get-tuple-element.78), channel_id=1, source_target_pairs={{0,12},{1,13},{2,14},{3,15},{4,8},{5,9},{6,10},{7,11},{8,4},{9,5},... | collective-permute-start | bytes 196616 | tf_op jit(solution)/shard_map/ppermute | solution.py:362
  58.7 15.9 %collective-permute-start.17 = (bf16[256,128]{1,0:T(8,128)(2,1)S(1)}, bf16[256,128]{1,0:T(8,128)(2,1)S(1)}, u32[]{:S(2)}, u32[]{:S(2)}) collective-permute-start(bf16[256,128]{1,0:T(8,128)(2,1)S(1)} %get-tuple-element.79), channel_id=1, source_target_pairs={{0,14},{1,15},{2,12},{3,13},{4,10},{5,11},{6,8},{7,9},{8,6},{9,7},... | collective-permute-start | bytes 196616 | tf_op jit(solution)/shard_map/ppermute | solution.py:362
  67.3 20.7 %collective-permute-start.3 = (bf16[256,128]{1,0:T(8,128)(2,1)S(1)}, bf16[256,128]{1,0:T(8,128)(2,1)S(1)}, u32[]{:S(2)}, u32[]{:S(2)}) collective-permute-start(bf16[256,128]{1,0:T(8,128)(2,1)S(1)} %get-tuple-element.60), channel_id=1, source_target_pairs={{0,24},{1,25},{2,26},{3,27},{4,28},{5,29},{6,30},{7,31},{8,16},{9,... | collective-permute-start | bytes 196616 | tf_op jit(solution)/shard_map/ppermute | solution.py:362
  69.6 10.0 %collective-permute-start.7 = (bf16[256,128]{1,0:T(8,128)(2,1)S(1)}, bf16[256,128]{1,0:T(8,128)(2,1)S(1)}, u32[]{:S(2)}, u32[]{:S(2)}) collective-permute-start(bf16[256,128]{1,0:T(8,128)(2,1)S(1)} %get-tuple-element.68), channel_id=1, source_target_pairs={{0,16},{1,17},{2,18},{3,19},{4,20},{5,21},{6,22},{7,23},{8,24},{9,... | collective-permute-start | bytes 196616 | tf_op jit(solution)/shard_map/ppermute | solution.py:362
  69.8 9.9 %collective-permute-start.8 = (bf16[256,128]{1,0:T(8,128)(2,1)S(1)}, bf16[256,128]{1,0:T(8,128)(2,1)S(1)}, u32[]{:S(2)}, u32[]{:S(2)}) collective-permute-start(bf16[256,128]{1,0:T(8,128)(2,1)S(1)} %get-tuple-element.69), channel_id=1, source_target_pairs={{0,18},{1,19},{2,16},{3,17},{4,22},{5,23},{6,20},{7,21},{8,26},{9,... | collective-permute-start | bytes 196616 | tf_op jit(solution)/shard_map/ppermute | solution.py:362
  69.8 15.1 %collective-permute-start.9 = (bf16[256,128]{1,0:T(8,128)(2,1)S(1)}, bf16[256,128]{1,0:T(8,128)(2,1)S(1)}, u32[]{:S(2)}, u32[]{:S(2)}) collective-permute-start(bf16[256,128]{1,0:T(8,128)(2,1)S(1)} %get-tuple-element.70), channel_id=1, source_target_pairs={{0,20},{1,21},{2,22},{3,23},{4,16},{5,17},{6,18},{7,19},{8,28},{9,... | collective-permute-start | bytes 196616 | tf_op jit(solution)/shard_map/ppermute | solution.py:362
  74.5 11.6 %collective-permute-start.10 = (bf16[256,128]{1,0:T(8,128)(2,1)S(1)}, bf16[256,128]{1,0:T(8,128)(2,1)S(1)}, u32[]{:S(2)}, u32[]{:S(2)}) collective-permute-start(bf16[256,128]{1,0:T(8,128)(2,1)S(1)} %get-tuple-element.71), channel_id=1, source_target_pairs={{0,22},{1,23},{2,20},{3,21},{4,18},{5,19},{6,16},{7,17},{8,30},{9,... | collective-permute-start | bytes 196616 | tf_op jit(solution)/shard_map/ppermute | solution.py:362
  79.6 8.5 %collective-permute-start.4 = (bf16[256,128]{1,0:T(8,128)(2,1)S(1)}, bf16[256,128]{1,0:T(8,128)(2,1)S(1)}, u32[]{:S(2)}, u32[]{:S(2)}) collective-permute-start(bf16[256,128]{1,0:T(8,128)(2,1)S(1)} %get-tuple-element.61), channel_id=1, source_target_pairs={{0,26},{1,27},{2,24},{3,25},{4,30},{5,31},{6,28},{7,29},{8,18},{9,... | collective-permute-start | bytes 196616 | tf_op jit(solution)/shard_map/ppermute | solution.py:362
  79.7 8.9 %collective-permute-start.5 = (bf16[256,128]{1,0:T(8,128)(2,1)S(1)}, bf16[256,128]{1,0:T(8,128)(2,1)S(1)}, u32[]{:S(2)}, u32[]{:S(2)}) collective-permute-start(bf16[256,128]{1,0:T(8,128)(2,1)S(1)} %get-tuple-element.62), channel_id=1, source_target_pairs={{0,28},{1,29},{2,30},{3,31},{4,24},{5,25},{6,26},{7,27},{8,20},{9,... | collective-permute-start | bytes 196616 | tf_op jit(solution)/shard_map/ppermute | solution.py:362
  84.9 7.9 %collective-permute-start.6 = (bf16[256,128]{1,0:T(8,128)(2,1)S(1)}, bf16[256,128]{1,0:T(8,128)(2,1)S(1)}, u32[]{:S(2)}, u32[]{:S(2)}) collective-permute-start(bf16[256,128]{1,0:T(8,128)(2,1)S(1)} %get-tuple-element.63), channel_id=1, source_target_pairs={{0,30},{1,31},{2,28},{3,29},{4,26},{5,27},{6,24},{7,25},{8,22},{9,... | collective-permute-start | bytes 196616 | tf_op jit(solution)/shard_map/ppermute | solution.py:362
where the time goes:
time: 96.6 us; the launch traced here: 96.2 us
  starting transfers between devices  41.8 us (43%)
  waiting for transfers between devices  25.7 us (27%)
  Pallas kernels  25 us (26%)
  between operations  2.7 us (3%)
  local copies, waits for them, and re-layouts  0.99 us (1%)
    ppermute x15, starting transfers between devices, body(): lax.ppermute(joined[j], axes, [(i, i ^ 2 * j) for i in range(devices)])  29.9 us
    ppermute x15, waiting for transfers between devices, body(): lax.ppermute(joined[j], axes, [(i, i ^ 2 * j) for i in range(devices)])  24 us
    pallas_call x3, Pallas kernels, body(): pl.pallas_call(functools.partial(rest_kernel, low, high, capacity0, parts...  8.56 us
    all_to_all x1, starting transfers between devices, body(): lax.all_to_all(everything, axes, split_axis=0, concat_axis=0, tiled=True)  7.34 us
    pallas_call x1, Pallas kernels, body(): pl.pallas_call(pack_kernel, out_shape=(pltpu.HBM((devices, capacity0 + ME...  6.83 us
    pallas_call x1, Pallas kernels, body(): pl.pallas_call(functools.partial(first_kernel, slots, parts), out_shape=(...  6.79 us
    ppermute x1, starting transfers between devices, halo(): above = lax.ppermute(shard[-EDGE:], axis, up)  3.04 us
    pallas_call x1, Pallas kernels, body(): pl.pallas_call(functools.partial(route_kernel, capacity), out_shape=(pltp...  2.76 us
  transfers between devices with their start and end apart: 19, of which 5 were waited for; matrix products, arithmetic and copies ran while one was open for 0% of the time, Pallas kernels for 15%

commit v1 on v0

--- a/solution.py
+++ b/solution.py
@@ -134,20 +134,29 @@
         copy.wait()
     wide = 2 * LANES
     tall = rows + 2 * EDGE
-    for c in range(cols // wide):
+    blocks = cols // wide
+    turn = rows // LANES
+
+    def vertical(c):
         part = jnp.dot(tv_ref[:, :tall], edged[:, c * wide : (c + 1) * wide], preferred_element_type=f32)
         vert[:, LANES + c * wide : LANES + (c + 1) * wide] = part.astype(bf16)
-    for c in range(cols // wide):
+
+    def horizontal(c):
         part = dot_last(vert[:, c * wide : c * wide + 2 * wide], th_ref[...])
         conv[2 * c * rows : (2 * c + 1) * rows, :] = part[:, :LANES]
         conv[(2 * c + 1) * rows : (2 * c + 2) * rows, :] = part[:, LANES:]
 
-    def scatter(r, carry):
-        for k, table in enumerate(tables):
-            spread[pl.ds(table[0, 0, r], 1), :] = conv[pl.ds(r + k * LANES, 1), :]
-        return carry
-
-    lax.fori_loop(0, LANES, scatter, 0, unroll=2)
+    vertical(0)
+    vertical(1)
+    horizontal(0)
+    for c in range(blocks):
+        if c + 2 < blocks:
+            vertical(c + 2)
+        if c + 1 < blocks:
+            horizontal(c + 1)
+        for k in range(2 * c * turn, 2 * (c + 1) * turn):
+            for r in range(LANES):
+                spread[pl.ds(tables[k][0, 0, r], 1), :] = conv[k * LANES + r : k * LANES + r + 1, :]
 
     def emit(k, carry):
         stage[k, :capacity0, :] = spread[pl.ds(pl.multiple_of(k * capacity, 8), capacity0), :].astype(bf16)
@@ -264,9 +273,10 @@
         return
     weight = weight_in[...]
 
+    inverse = 1.0 / jnp.maximum(weight, 1.0)
+
     def mean(h, total):
-        scale = jnp.broadcast_to(jnp.maximum(weight[h : h + 1, :], 1.0), (LANES, LANES)).T
-        return total / scale
+        return total * jnp.broadcast_to(inverse[h : h + 1, :], (LANES, LANES)).T
 
     merge(sums, stage, mean, image_ref, sems)
 

time: 96.6 us -> 95.9 us (level)
  no operation moved by 1% of the time
where the time goes in v1:
time: 95.9 us; the launch traced here: 95.6 us
  starting transfers between devices  41.8 us (44%)
  waiting for transfers between devices  25.7 us (27%)
  Pallas kernels  24.3 us (25%)
  between operations  2.7 us (3%)
  local copies, waits for them, and re-layouts  0.99 us (1%)
    ppermute x15, starting transfers between devices, body(): lax.ppermute(joined[j], axes, [(i, i ^ 2 * j) for i in range(devices)])  29.9 us
    ppermute x15, waiting for transfers between devices, body(): lax.ppermute(joined[j], axes, [(i, i ^ 2 * j) for i in range(devices)])  24 us
    pallas_call x3, Pallas kernels, body(): pl.pallas_call(functools.partial(rest_kernel, low, high, capacity0, parts...  8.6 us
    all_to_all x1, starting transfers between devices, body(): lax.all_to_all(everything, axes, split_axis=0, concat_axis=0, tiled=True)  7.33 us
    pallas_call x1, Pallas kernels, body(): pl.pallas_call(functools.partial(first_kernel, slots, parts), out_shape=(...  6.79 us
    pallas_call x1, Pallas kernels, body(): pl.pallas_call(pack_kernel, out_shape=(pltpu.HBM((devices, capacity0 + ME...  6.12 us
    ppermute x1, starting transfers between devices, halo(): above = lax.ppermute(shard[-EDGE:], axis, up)  3.04 us
    pallas_call x1, Pallas kernels, body(): pl.pallas_call(functools.partial(route_kernel, capacity), out_shape=(pltp...  2.76 us
  transfers between devices with their start and end apart: 19, of which 5 were waited for; matrix products, arithmetic and copies ran while one was open for 0% of the time, Pallas kernels for 15%

profile of v1, /device:TPU:0, one launch (start us, length us, event | category | flops | bytes accessed | tf_op | source)
XLA Modules:
  0.0 95.6 jit_solution(11828515077099577040)
XLA Ops:
  0.6 1.0 %slice_bitcast_fusion = (bf16[32,2048]{1,0:T(8,128)(2,1)S(1)}, bf16[32,2048]{1,0:T(8,128)(2,1)S(1)}) fusion(bf16[1,256,2048]{2,1,0:T(8,128)(2,1)} %param.7), kind=kLoop, calls=%fused_computation | loop fusion | bytes 524288 | tf_op jit(solution)/shard_map/slice | solution.py:52
  1.6 1.3 %collective-permute-start.1 = (bf16[32,2048]{1,0:T(8,128)(2,1)S(1)}, bf16[32,2048]{1,0:T(8,128)(2,1)S(1)}, u32[]{:S(2)}, u32[]{:S(2)}) collective-permute-start(bf16[32,2048]{1,0:T(8,128)(2,1)S(1)} %get-tuple-element.106), channel_id=1, source_target_pairs={{1,0},{2,1},{3,2},{4,3},{5,4},{6,5},{7,6},{9,8},{10,9},{11,10},{12... | collective-permute-start | bytes 393224 | tf_op jit(solution)/shard_map/ppermute | solution.py:52
  2.9 3.0 %collective-permute-start = (bf16[32,2048]{1,0:T(8,128)(2,1)S(1)}, bf16[32,2048]{1,0:T(8,128)(2,1)S(1)}, u32[]{:S(2)}, u32[]{:S(2)}) collective-permute-start(bf16[32,2048]{1,0:T(8,128)(2,1)S(1)} %get-tuple-element.107), channel_id=1, source_target_pairs={{0,1},{1,2},{2,3},{3,4},{4,5},{5,6},{6,7},{8,9},{9,10},{10,11},{11... | collective-permute-start | bytes 393224 | tf_op jit(solution)/shard_map/ppermute | solution.py:51
  7.9 2.8 %route.1 = (s32[32,1,128]{2,1,0:T(1,128)S(1)}, bf16[256,128]{1,0:T(8,128)(2,1)S(1)}, bf16[256,384]{1,0:T(8,128)(2,1)S(1)}, bf16[256,512]{1,0:T(8,128)(2,1)S(1)}) custom-call(s32[16,1,256]{2,1,0:T(1,128)} %bitcast.15, s32[16,256]{1,0:T(8,128)} %bitcast.16, s32[1,1]{1,0:T(1,128)S(6)} %copy.59.gap_ref, f32[1,1]{1,0:T(1,128)S(6)} %copy.58.var_ref, ...), custom_call_target="tpu_custom_call" | custom-call | flops 400000000 | bytes 600000 | tf_op jit(solution)/shard_map/route/pallas_call | solution.py:316
  10.7 0.0 collective-permute-done.1.below_ref
  10.7 0.0 collective-permute-done.above_ref
  10.7 6.1 %pack.1 = (bf16[32,136,128]{2,1,0:T(8,128)(2,1)}, bf16[16,128,128]{2,1,0:T(8,128)(2,1)S(1)}, bf16[16,128,128]{2,1,0:T(8,128)(2,1)S(1)}) custom-call(bf16[256,2048]{1,0:T(8,128)(2,1)} %bitcast.13, bf16[32,2048]{1,0:T(8,128)(2,1)S(1)} %collective-permute-done.above_ref, bf16[32,2048]{1,0:T(8,128)(2,1)S(1)} %collective-permute-done.1.below_ref, ...), custom_call_target="tpu_custom_call" | custom-call | flops 10000000000 | bytes 4000000 | tf_op jit(solution)/shard_map/pack/pallas_call | solution.py:335
  16.8 7.3 %all-to-all-start = ((bf16[32,136,128]{2,1,0:T(8,128)(2,1)}), bf16[32,136,128]{2,1,0:T(8,128)(2,1)S(1)}, u32[]{:S(2)}, u32[]{:S(2)}) async-start(bf16[32,136,128]{2,1,0:T(8,128)(2,1)} %get-tuple-element.64), calls=%async_computation | async-start | bytes 2228224 | tf_op jit(solution)/shard_map/all_to_all | solution.py:357
  24.2 0.3 collective-permute-start.2
  24.5 1.7 %collective-permute-done.2.take_ref = bf16[16,128,128]{2,1,0:T(8,128)(2,1)S(1)} collective-permute-done((bf16[16,128,128]{2,1,0:T(8,128)(2,1)S(1)}, bf16[16,128,128]{2,1,0:T(8,128)(2,1)S(1)}, u32[]{:S(2)}, u32[]{:S(2)}) %collective-permute-start.2) | collective-permute-done | bytes 524320 | tf_op jit(solution)/shard_map/ppermute | solution.py:358
  26.1 0.1 join.1
  26.2 1.8 %collective-permute-start.11 = (bf16[256,128]{1,0:T(8,128)(2,1)S(1)}, bf16[256,128]{1,0:T(8,128)(2,1)S(1)}, u32[]{:S(2)}, u32[]{:S(2)}) collective-permute-start(bf16[256,128]{1,0:T(8,128)(2,1)S(1)} %get-tuple-element.73), channel_id=1, source_target_pairs={{0,2},{1,3},{2,0},{3,1},{4,6},{5,7},{6,4},{7,5},{8,10},{9,11},{10,... | collective-permute-start | bytes 196616 | tf_op jit(solution)/shard_map/ppermute | solution.py:372
  28.1 2.4 %collective-permute-start.12 = (bf16[256,128]{1,0:T(8,128)(2,1)S(1)}, bf16[256,128]{1,0:T(8,128)(2,1)S(1)}, u32[]{:S(2)}, u32[]{:S(2)}) collective-permute-start(bf16[256,128]{1,0:T(8,128)(2,1)S(1)} %get-tuple-element.74), channel_id=1, source_target_pairs={{0,4},{1,5},{2,6},{3,7},{4,0},{5,1},{6,2},{7,3},{8,12},{9,13},{10,... | collective-permute-start | bytes 196616 | tf_op jit(solution)/shard_map/ppermute | solution.py:372
  30.5 0.2 collective-permute-start.13
  30.7 1.8 %collective-permute-start.14 = (bf16[256,128]{1,0:T(8,128)(2,1)S(1)}, bf16[256,128]{1,0:T(8,128)(2,1)S(1)}, u32[]{:S(2)}, u32[]{:S(2)}) collective-permute-start(bf16[256,128]{1,0:T(8,128)(2,1)S(1)} %get-tuple-element.76), channel_id=1, source_target_pairs={{0,8},{1,9},{2,10},{3,11},{4,12},{5,13},{6,14},{7,15},{8,0},{9,1},... | collective-permute-start | bytes 196616 | tf_op jit(solution)/shard_map/ppermute | solution.py:372
  32.4 0.6 collective-permute-start.15
  33.0 11.5 %collective-permute-done.11.refs_1_ = bf16[256,128]{1,0:T(8,128)(2,1)S(1)} collective-permute-done((bf16[256,128]{1,0:T(8,128)(2,1)S(1)}, bf16[256,128]{1,0:T(8,128)(2,1)S(1)}, u32[]{:S(2)}, u32[]{:S(2)}) %collective-permute-start.11) | collective-permute-done | bytes 65568 | tf_op jit(solution)/shard_map/ppermute | solution.py:372
  44.5 5.7 %collective-permute-start.16 = (bf16[256,128]{1,0:T(8,128)(2,1)S(1)}, bf16[256,128]{1,0:T(8,128)(2,1)S(1)}, u32[]{:S(2)}, u32[]{:S(2)}) collective-permute-start(bf16[256,128]{1,0:T(8,128)(2,1)S(1)} %get-tuple-element.78), channel_id=1, source_target_pairs={{0,12},{1,13},{2,14},{3,15},{4,8},{5,9},{6,10},{7,11},{8,4},{9,5},... | collective-permute-start | bytes 196616 | tf_op jit(solution)/shard_map/ppermute | solution.py:372
  50.2 7.8 %collective-permute-done.12.refs_2_ = bf16[256,128]{1,0:T(8,128)(2,1)S(1)} collective-permute-done((bf16[256,128]{1,0:T(8,128)(2,1)S(1)}, bf16[256,128]{1,0:T(8,128)(2,1)S(1)}, u32[]{:S(2)}, u32[]{:S(2)}) %collective-permute-start.12) | collective-permute-done | bytes 65568 | tf_op jit(solution)/shard_map/ppermute | solution.py:372
  58.0 1.8 %collective-permute-start.17 = (bf16[256,128]{1,0:T(8,128)(2,1)S(1)}, bf16[256,128]{1,0:T(8,128)(2,1)S(1)}, u32[]{:S(2)}, u32[]{:S(2)}) collective-permute-start(bf16[256,128]{1,0:T(8,128)(2,1)S(1)} %get-tuple-element.79), channel_id=1, source_target_pairs={{0,14},{1,15},{2,12},{3,13},{4,10},{5,11},{6,8},{7,9},{8,6},{9,7},... | collective-permute-start | bytes 196616 | tf_op jit(solution)/shard_map/ppermute | solution.py:372
  59.8 0.0 all-to-all-done.values_ref
  59.8 6.8 %sum_first.1 = (s32[64,1,128]{2,1,0:T(1,128)S(1)}, f32[32,1,128]{2,1,0:T(1,128)S(1)}, f32[32,128]{1,0:T(8,128)S(1)}, f32[4352,128]{1,0:T(8,128)S(1)}, f32[4352,1...) custom-call(bf16[32,136,128]{2,1,0:T(8,128)(2,1)S(1)} %all-to-all-do, ...), custom_call_target="tpu_custom_call" | custom-call | flops 4000000000 | bytes 8000000 | tf_op jit(solution)/shard_map/sum_first/pallas_call | solution.py:375
  66.6 0.0 collective-permute-done.13.refs_3_
  66.6 2.2 %collective-permute-start.3 = (bf16[256,128]{1,0:T(8,128)(2,1)S(1)}, bf16[256,128]{1,0:T(8,128)(2,1)S(1)}, u32[]{:S(2)}, u32[]{:S(2)}) collective-permute-start(bf16[256,128]{1,0:T(8,128)(2,1)S(1)} %get-tuple-element.60), channel_id=1, source_target_pairs={{0,24},{1,25},{2,26},{3,27},{4,28},{5,29},{6,30},{7,31},{8,16},{9,... | collective-permute-start | bytes 196616 | tf_op jit(solution)/shard_map/ppermute | solution.py:372
  68.9 0.0 collective-permute-done.14.refs_4_
  68.9 0.2 collective-permute-start.7
  69.1 0.0 collective-permute-done.15.refs_5_
  69.1 0.0 collective-permute-start.8
  69.1 0.0 collective-permute-done.16.refs_6_
  69.1 4.7 %collective-permute-start.9 = (bf16[256,128]{1,0:T(8,128)(2,1)S(1)}, bf16[256,128]{1,0:T(8,128)(2,1)S(1)}, u32[]{:S(2)}, u32[]{:S(2)}) collective-permute-start(bf16[256,128]{1,0:T(8,128)(2,1)S(1)} %get-tuple-element.70), channel_id=1, source_target_pairs={{0,20},{1,21},{2,22},{3,23},{4,16},{5,17},{6,18},{7,19},{8,28},{9,... | collective-permute-start | bytes 196616 | tf_op jit(solution)/shard_map/ppermute | solution.py:372
  73.8 0.0 collective-permute-done.17.refs_7_
  73.8 1.8 %collective-permute-start.10 = (bf16[256,128]{1,0:T(8,128)(2,1)S(1)}, bf16[256,128]{1,0:T(8,128)(2,1)S(1)}, u32[]{:S(2)}, u32[]{:S(2)}) collective-permute-start(bf16[256,128]{1,0:T(8,128)(2,1)S(1)} %get-tuple-element.71), channel_id=1, source_target_pairs={{0,22},{1,23},{2,20},{3,21},{4,18},{5,19},{6,16},{7,17},{8,30},{9,... | collective-permute-start | bytes 196616 | tf_op jit(solution)/shard_map/ppermute | solution.py:372
  75.6 3.3 %shard_map.86 = (f32[4352,128]{1,0:T(8,128)S(1)}, f32[4352,128]{1,0:T(8,128)S(1)}, f32[4352,128]{1,0:T(8,128)S(1)}, f32[4352,128]{1,0:T(8,128)S(1)}, f32[4352,12...) custom-call(bf16[256,128]{1,0:T(8,128)(2,1)S(1)} %get-tuple-element., ...), custom_call_target="tpu_custom_call", output_to_operand_aliasing={{0}: (10, {}), {1}: (11, {}), {2}: (12, {}), {3}: (13, {}),... | custom-call | flops 4000000000 | bytes 8000000 | tf_op jit(solution)/shard_map/pallas_call | solution.py:401
  78.9 0.0 collective-permute-done.7.refs_0_
  78.9 0.1 collective-permute-start.4
  79.0 0.0 collective-permute-done.8.refs_1_
  79.0 5.2 %collective-permute-start.5 = (bf16[256,128]{1,0:T(8,128)(2,1)S(1)}, bf16[256,128]{1,0:T(8,128)(2,1)S(1)}, u32[]{:S(2)}, u32[]{:S(2)}) collective-permute-start(bf16[256,128]{1,0:T(8,128)(2,1)S(1)} %get-tuple-element.62), channel_id=1, source_target_pairs={{0,28},{1,29},{2,30},{3,31},{4,24},{5,25},{6,26},{7,27},{8,20},{9,... | collective-permute-start | bytes 196616 | tf_op jit(solution)/shard_map/ppermute | solution.py:372
  84.2 0.0 collective-permute-done.9.refs_2_
  84.2 1.3 %collective-permute-start.6 = (bf16[256,128]{1,0:T(8,128)(2,1)S(1)}, bf16[256,128]{1,0:T(8,128)(2,1)S(1)}, u32[]{:S(2)}, u32[]{:S(2)}) collective-permute-start(bf16[256,128]{1,0:T(8,128)(2,1)S(1)} %get-tuple-element.63), channel_id=1, source_target_pairs={{0,30},{1,31},{2,28},{3,29},{4,26},{5,27},{6,24},{7,25},{8,22},{9,... | collective-permute-start | bytes 196616 | tf_op jit(solution)/shard_map/ppermute | solution.py:372
  85.5 0.0 collective-permute-done.10.refs_3_
  85.5 1.9 %shard_map.87 = (f32[4352,128]{1,0:T(8,128)S(1)}, f32[4352,128]{1,0:T(8,128)S(1)}, f32[4352,128]{1,0:T(8,128)S(1)}, f32[4352,128]{1,0:T(8,128)S(1)}, f32[4352,12...) custom-call(bf16[256,128]{1,0:T(8,128)(2,1)S(1)} %collective-permute, ...), custom_call_target="tpu_custom_call", output_to_operand_aliasing={{0}: (6, {}), {1}: (7, {}), {2}: (8, {}), {3}: (9, {}), {4}... | custom-call | flops 4000000000 | bytes 8000000 | tf_op jit(solution)/shard_map/pallas_call | solution.py:401
  87.3 0.0 collective-permute-done.3.refs_0_
  87.3 0.0 collective-permute-done.4.refs_1_
  87.3 0.5 collective-permute-done.5.refs_2_
  87.8 4.2 %collective-permute-done.6.refs_3_ = bf16[256,128]{1,0:T(8,128)(2,1)S(1)} collective-permute-done((bf16[256,128]{1,0:T(8,128)(2,1)S(1)}, bf16[256,128]{1,0:T(8,128)(2,1)S(1)}, u32[]{:S(2)}, u32[]{:S(2)}) %collective-permute-start.6) | collective-permute-done | bytes 65568 | tf_op jit(solution)/shard_map/ppermute | solution.py:372
  92.1 3.5 %shard_map.88 = (f32[4096,128]{1,0:T(8,128)}, f32[32,128]{1,0:T(8,128)}, f32[4352,128]{1,0:T(8,128)S(1)}, f32[4352,128]{1,0:T(8,128)S(1)}, f32[4352,128]{1,0:T(8...) custom-call(bf16[256,128]{1,0:T(8,128)(2,1)S(1)} %collective-permute, ...), custom_call_target="tpu_custom_call", output_to_operand_aliasing={{2}: (7, {}), {3}: (8, {}), {4}: (9, {}), {5}: (10, {}), {6... | custom-call | flops 4000000000 | bytes 8000000 | tf_op jit(solution)/shard_map/pallas_call | solution.py:401
Async XLA Ops:
  1.6 9.1 %collective-permute-start.1 = (bf16[32,2048]{1,0:T(8,128)(2,1)S(1)}, bf16[32,2048]{1,0:T(8,128)(2,1)S(1)}, u32[]{:S(2)}, u32[]{:S(2)}) collective-permute-start(bf16[32,2048]{1,0:T(8,128)(2,1)S(1)} %get-tuple-element.106), channel_id=1, source_target_pairs={{1,0},{2,1},{3,2},{4,3},{5,4},{6,5},{7,6},{9,8},{10,9},{11,10},{12... | collective-permute-start | bytes 393224 | tf_op jit(solution)/shard_map/ppermute | solution.py:52
  2.9 7.8 %collective-permute-start = (bf16[32,2048]{1,0:T(8,128)(2,1)S(1)}, bf16[32,2048]{1,0:T(8,128)(2,1)S(1)}, u32[]{:S(2)}, u32[]{:S(2)}) collective-permute-start(bf16[32,2048]{1,0:T(8,128)(2,1)S(1)} %get-tuple-element.107), channel_id=1, source_target_pairs={{0,1},{1,2},{2,3},{3,4},{4,5},{5,6},{6,7},{8,9},{9,10},{10,11},{11... | collective-permute-start | bytes 393224 | tf_op jit(solution)/shard_map/ppermute | solution.py:51
  16.8 43.0 %all-to-all-start = ((bf16[32,136,128]{2,1,0:T(8,128)(2,1)}), bf16[32,136,128]{2,1,0:T(8,128)(2,1)S(1)}, u32[]{:S(2)}, u32[]{:S(2)}) async-start(bf16[32,136,128]{2,1,0:T(8,128)(2,1)} %get-tuple-element.64), calls=%async_computation | async-start | bytes 2228224 | tf_op jit(solution)/shard_map/all_to_all | solution.py:357
  24.2 2.0 %collective-permute-start.2 = (bf16[16,128,128]{2,1,0:T(8,128)(2,1)S(1)}, bf16[16,128,128]{2,1,0:T(8,128)(2,1)S(1)}, u32[]{:S(2)}, u32[]{:S(2)}) collective-permute-start(bf16[16,128,128]{2,1,0:T(8,128)(2,1)S(1)} %get-tuple-element.59), channel_id=1, source_target_pairs={{0,1},{1,0},{2,3},{3,2},{4,5},{5,4},{6,7},{7,6},{8,9},{9,8},{10,11... | collective-permute-start | bytes 1572872 | tf_op jit(solution)/shard_map/ppermute | solution.py:358
  26.2 18.3 %collective-permute-start.11 = (bf16[256,128]{1,0:T(8,128)(2,1)S(1)}, bf16[256,128]{1,0:T(8,128)(2,1)S(1)}, u32[]{:S(2)}, u32[]{:S(2)}) collective-permute-start(bf16[256,128]{1,0:T(8,128)(2,1)S(1)} %get-tuple-element.73), channel_id=1, source_target_pairs={{0,2},{1,3},{2,0},{3,1},{4,6},{5,7},{6,4},{7,5},{8,10},{9,11},{10,... | collective-permute-start | bytes 196616 | tf_op jit(solution)/shard_map/ppermute | solution.py:372
  28.1 29.9 %collective-permute-start.12 = (bf16[256,128]{1,0:T(8,128)(2,1)S(1)}, bf16[256,128]{1,0:T(8,128)(2,1)S(1)}, u32[]{:S(2)}, u32[]{:S(2)}) collective-permute-start(bf16[256,128]{1,0:T(8,128)(2,1)S(1)} %get-tuple-element.74), channel_id=1, source_target_pairs={{0,4},{1,5},{2,6},{3,7},{4,0},{5,1},{6,2},{7,3},{8,12},{9,13},{10,... | collective-permute-start | bytes 196616 | tf_op jit(solution)/shard_map/ppermute | solution.py:372
  30.5 36.1 %collective-permute-start.13 = (bf16[256,128]{1,0:T(8,128)(2,1)S(1)}, bf16[256,128]{1,0:T(8,128)(2,1)S(1)}, u32[]{:S(2)}, u32[]{:S(2)}) collective-permute-start(bf16[256,128]{1,0:T(8,128)(2,1)S(1)} %get-tuple-element.75), channel_id=1, source_target_pairs={{0,6},{1,7},{2,4},{3,5},{4,2},{5,3},{6,0},{7,1},{8,14},{9,15},{10,... | collective-permute-start | bytes 196616 | tf_op jit(solution)/shard_map/ppermute | solution.py:372
  30.7 38.2 %collective-permute-start.14 = (bf16[256,128]{1,0:T(8,128)(2,1)S(1)}, bf16[256,128]{1,0:T(8,128)(2,1)S(1)}, u32[]{:S(2)}, u32[]{:S(2)}) collective-permute-start(bf16[256,128]{1,0:T(8,128)(2,1)S(1)} %get-tuple-element.76), channel_id=1, source_target_pairs={{0,8},{1,9},{2,10},{3,11},{4,12},{5,13},{6,14},{7,15},{8,0},{9,1},... | collective-permute-start | bytes 196616 | tf_op jit(solution)/shard_map/ppermute | solution.py:372
  32.4 36.6 %collective-permute-start.15 = (bf16[256,128]{1,0:T(8,128)(2,1)S(1)}, bf16[256,128]{1,0:T(8,128)(2,1)S(1)}, u32[]{:S(2)}, u32[]{:S(2)}) collective-permute-start(bf16[256,128]{1,0:T(8,128)(2,1)S(1)} %get-tuple-element.77), channel_id=1, source_target_pairs={{0,10},{1,11},{2,8},{3,9},{4,14},{5,15},{6,12},{7,13},{8,2},{9,3},... | collective-permute-start | bytes 196616 | tf_op jit(solution)/shard_map/ppermute | solution.py:372
  44.5 24.6 %collective-permute-start.16 = (bf16[256,128]{1,0:T(8,128)(2,1)S(1)}, bf16[256,128]{1,0:T(8,128)(2,1)S(1)}, u32[]{:S(2)}, u32[]{:S(2)}) collective-permute-start(bf16[256,128]{1,0:T(8,128)(2,1)S(1)} %get-tuple-element.78), channel_id=1, source_target_pairs={{0,12},{1,13},{2,14},{3,15},{4,8},{5,9},{6,10},{7,11},{8,4},{9,5},... | collective-permute-start | bytes 196616 | tf_op jit(solution)/shard_map/ppermute | solution.py:372
  58.0 15.9 %collective-permute-start.17 = (bf16[256,128]{1,0:T(8,128)(2,1)S(1)}, bf16[256,128]{1,0:T(8,128)(2,1)S(1)}, u32[]{:S(2)}, u32[]{:S(2)}) collective-permute-start(bf16[256,128]{1,0:T(8,128)(2,1)S(1)} %get-tuple-element.79), channel_id=1, source_target_pairs={{0,14},{1,15},{2,12},{3,13},{4,10},{5,11},{6,8},{7,9},{8,6},{9,7},... | collective-permute-start | bytes 196616 | tf_op jit(solution)/shard_map/ppermute | solution.py:372
  66.6 20.7 %collective-permute-start.3 = (bf16[256,128]{1,0:T(8,128)(2,1)S(1)}, bf16[256,128]{1,0:T(8,128)(2,1)S(1)}, u32[]{:S(2)}, u32[]{:S(2)}) collective-permute-start(bf16[256,128]{1,0:T(8,128)(2,1)S(1)} %get-tuple-element.60), channel_id=1, source_target_pairs={{0,24},{1,25},{2,26},{3,27},{4,28},{5,29},{6,30},{7,31},{8,16},{9,... | collective-permute-start | bytes 196616 | tf_op jit(solution)/shard_map/ppermute | solution.py:372
  68.9 10.0 %collective-permute-start.7 = (bf16[256,128]{1,0:T(8,128)(2,1)S(1)}, bf16[256,128]{1,0:T(8,128)(2,1)S(1)}, u32[]{:S(2)}, u32[]{:S(2)}) collective-permute-start(bf16[256,128]{1,0:T(8,128)(2,1)S(1)} %get-tuple-element.68), channel_id=1, source_target_pairs={{0,16},{1,17},{2,18},{3,19},{4,20},{5,21},{6,22},{7,23},{8,24},{9,... | collective-permute-start | bytes 196616 | tf_op jit(solution)/shard_map/ppermute | solution.py:372
  69.1 9.9 %collective-permute-start.8 = (bf16[256,128]{1,0:T(8,128)(2,1)S(1)}, bf16[256,128]{1,0:T(8,128)(2,1)S(1)}, u32[]{:S(2)}, u32[]{:S(2)}) collective-permute-start(bf16[256,128]{1,0:T(8,128)(2,1)S(1)} %get-tuple-element.69), channel_id=1, source_target_pairs={{0,18},{1,19},{2,16},{3,17},{4,22},{5,23},{6,20},{7,21},{8,26},{9,... | collective-permute-start | bytes 196616 | tf_op jit(solution)/shard_map/ppermute | solution.py:372
  69.1 15.1 %collective-permute-start.9 = (bf16[256,128]{1,0:T(8,128)(2,1)S(1)}, bf16[256,128]{1,0:T(8,128)(2,1)S(1)}, u32[]{:S(2)}, u32[]{:S(2)}) collective-permute-start(bf16[256,128]{1,0:T(8,128)(2,1)S(1)} %get-tuple-element.70), channel_id=1, source_target_pairs={{0,20},{1,21},{2,22},{3,23},{4,16},{5,17},{6,18},{7,19},{8,28},{9,... | collective-permute-start | bytes 196616 | tf_op jit(solution)/shard_map/ppermute | solution.py:372
  73.8 11.6 %collective-permute-start.10 = (bf16[256,128]{1,0:T(8,128)(2,1)S(1)}, bf16[256,128]{1,0:T(8,128)(2,1)S(1)}, u32[]{:S(2)}, u32[]{:S(2)}) collective-permute-start(bf16[256,128]{1,0:T(8,128)(2,1)S(1)} %get-tuple-element.71), channel_id=1, source_target_pairs={{0,22},{1,23},{2,20},{3,21},{4,18},{5,19},{6,16},{7,17},{8,30},{9,... | collective-permute-start | bytes 196616 | tf_op jit(solution)/shard_map/ppermute | solution.py:372
  78.9 8.5 %collective-permute-start.4 = (bf16[256,128]{1,0:T(8,128)(2,1)S(1)}, bf16[256,128]{1,0:T(8,128)(2,1)S(1)}, u32[]{:S(2)}, u32[]{:S(2)}) collective-permute-start(bf16[256,128]{1,0:T(8,128)(2,1)S(1)} %get-tuple-element.61), channel_id=1, source_target_pairs={{0,26},{1,27},{2,24},{3,25},{4,30},{5,31},{6,28},{7,29},{8,18},{9,... | collective-permute-start | bytes 196616 | tf_op jit(solution)/shard_map/ppermute | solution.py:372
  79.0 8.9 %collective-permute-start.5 = (bf16[256,128]{1,0:T(8,128)(2,1)S(1)}, bf16[256,128]{1,0:T(8,128)(2,1)S(1)}, u32[]{:S(2)}, u32[]{:S(2)}) collective-permute-start(bf16[256,128]{1,0:T(8,128)(2,1)S(1)} %get-tuple-element.62), channel_id=1, source_target_pairs={{0,28},{1,29},{2,30},{3,31},{4,24},{5,25},{6,26},{7,27},{8,20},{9,... | collective-permute-start | bytes 196616 | tf_op jit(solution)/shard_map/ppermute | solution.py:372
  84.2 7.9 %collective-permute-start.6 = (bf16[256,128]{1,0:T(8,128)(2,1)S(1)}, bf16[256,128]{1,0:T(8,128)(2,1)S(1)}, u32[]{:S(2)}, u32[]{:S(2)}) collective-permute-start(bf16[256,128]{1,0:T(8,128)(2,1)S(1)} %get-tuple-element.63), channel_id=1, source_target_pairs={{0,30},{1,31},{2,28},{3,29},{4,26},{5,27},{6,24},{7,25},{8,22},{9,... | collective-permute-start | bytes 196616 | tf_op jit(solution)/shard_map/ppermute | solution.py:372
